TPU v7x, 256 devices: a whole 4x4x8 slice. The times are simulated.
256 devices in a mesh: req: 32 (over z_lo, x, y), tp: 8 (over z_hi, core).
Axes of the slice: x: 4, y: 4, z: 8 (z_hi: 4, z_lo: 2; z = z_hi * 2 + z_lo), core: 2. Of those that a mesh axis runs over, the one named last changes fastest.
Arguments:
- queries: bfloat16 [32768, 5120], P('req', 'tp')
- keys: bfloat16 [32768, 5120], P('req', 'tp')
- values: bfloat16 [32768, 5120], P('req', 'tp'), may hold values from -6 to 6
- cross_queries: bfloat16 [32768, 5120], P('req', 'tp')
- text_kv: bfloat16 [1024, 2, 5120], P(('req', 'tp'))
- segment_ids: int32 [32, 1024], P('req'), may hold values from 0 to 5, never falling along the last dimension, each value on 1 to 682 neighbouring positions
- prompt_of: int32 [32], P('req'), may hold values from 0 to 1
- page_owner: int32 [2048, 1], P('req'), may hold values from 0 to 31; in each aligned block of 64 rows (0 to 63, 64 to 127, ...) at most 3 rows name the same one
Outputs:
- self_out: bfloat16 [32768, 5120], P('req', 'tp')
- cross_out: bfloat16 [32768, 5120], P('req', 'tp')
- cache: bfloat16 [49152, 2, 5120], P('req', None, 'tp')
Inputs may be any that keep to these rules, and one draw needn't show every extreme that they name: `page_owner`: among the pages of one stream (an aligned block of 64 rows), no device index appears more than 3 times; in some streams one appears exactly 3 times.
All inputs are finite; a program needn't handle non-finite values.
Results may differ from a plain program's by a relative error of at most 0.003.
The roundings to bfloat16 on the way count: a program that leaves them out, or rounds other values in their place, can miss the bound.
Values may be sent and summed in bfloat16 or wider, within the bound.
A program may use at most 128 MiB of HBM per device.

v0:
```python
import math

import jax
import jax.numpy as jnp
from jax import lax
from jax.sharding import PartitionSpec as P

HEADS = 40
HEAD = 128
TEXT = 512
PAGE = 16


EPSILON = 1e-06
NEGATIVE = -1e30


def square_sums(block):
    wide = block.astype(jnp.float32)
    return jnp.sum(wide * wide, axis=1)


def scaled_rows(block, totals, width):
    factor = lax.rsqrt(totals / width + EPSILON)
    return (block.astype(jnp.float32) * factor[:, None]).astype(jnp.bfloat16)


def empty_state(heads, count, depth):
    return (
        jnp.full((heads, count), NEGATIVE, jnp.float32),
        jnp.zeros((heads, count), jnp.float32),
        jnp.zeros((heads, count, depth), jnp.float32),
    )


def blend(state, scores, allowed, value_part):
    running_max, running_sum, accum = state
    masked = jnp.where(allowed, scores, NEGATIVE)
    new_max = jnp.maximum(running_max, jnp.max(masked, axis=2))
    weights = jnp.where(allowed, jnp.exp(masked - new_max[:, :, None]), 0.0)
    new_sum = jnp.sum(weights, axis=2)
    product = jnp.einsum(
        "hqk,khe->hqe", weights.astype(jnp.bfloat16), value_part, preferred_element_type=jnp.float32
    )
    return (new_max, new_sum, product)


def finish(state):
    return state[2] / state[1][:, :, None]


def attend_block(state, query_part, query_seg, key_part, value_part, key_seg, scale):
    scores = (
        jnp.einsum("qhe,khe->hqk", query_part, key_part, preferred_element_type=jnp.float32) * scale
    )
    allowed = (query_seg[:, None] == key_seg[None, :])[None]
    return blend(state, scores, allowed, value_part)


def self_attention(query_heads, key_heads, value_heads, segments):
    length, heads, depth = query_heads.shape
    block = math.gcd(length, 512)
    scale = depth ** (-0.5)
    results = []
    for query_start in range(0, length, block):
        query_part = query_heads[query_start : query_start + block]
        query_seg = segments[query_start : query_start + block]
        state = empty_state(heads, block, depth)
        state = attend_block(state, query_part, query_seg, key_heads, value_heads, segments, scale)
        results.append(finish(state))
    joined = jnp.concatenate(results, axis=1)
    return joined.transpose(1, 0, 2).reshape(length, heads * depth).astype(jnp.bfloat16)


def cross_attention(cross_heads, prompt_rows):
    length, heads, depth = cross_heads.shape
    count = prompt_rows.shape[0]
    key_part = prompt_rows[:, 0, :].reshape(count, heads, depth)
    value_part = prompt_rows[:, 1, :].reshape(count, heads, depth)
    block = math.gcd(length, 512)
    scale = depth ** (-0.5)
    everywhere = jnp.ones((1, 1, count), dtype=jnp.bool_)
    results = []
    for query_start in range(0, length, block):
        query_part = cross_heads[query_start : query_start + block]
        scores = (
            jnp.einsum("qhe,khe->hqk", query_part, key_part, preferred_element_type=jnp.float32)
            * scale
        )
        state = blend(empty_state(heads, block, depth), scores, everywhere, value_part)
        results.append(finish(state))
    joined = jnp.concatenate(results, axis=1)
    return joined.transpose(1, 0, 2).reshape(length, heads * depth).astype(jnp.bfloat16)


def per_device(queries, keys, values, cross_queries, text_kv, segment_ids, prompt_of, page_owner):
    width = HEADS * HEAD
    stream = queries.shape[0]
    width_dev = queries.shape[1]
    heads_dev = width_dev // HEAD
    query_total, key_total, cross_total = lax.psum(
        (square_sums(queries), square_sums(keys), square_sums(cross_queries)), "tp"
    )
    query_hat = scaled_rows(queries, query_total, width)
    key_hat = scaled_rows(keys, key_total, width)
    cross_hat = scaled_rows(cross_queries, cross_total, width)
    text_keys = text_kv[:, 0, :]
    text_hat = scaled_rows(text_keys, square_sums(text_keys), width)
    text_ready = jnp.stack([text_hat, text_kv[:, 1, :]], axis=1)
    nreq = lax.axis_size("req")
    pages = stream // PAGE
    capacity = max(2, (3 * pages + 2 * nreq - 1) // (2 * nreq))
    owners = page_owner[:, 0]
    same_owner = owners[:, None] == owners[None, :]
    before = lax.broadcasted_iota(jnp.int32, (pages, pages), 1) < lax.broadcasted_iota(
        jnp.int32, (pages, pages), 0
    )
    rank = jnp.sum(jnp.where(jnp.logical_and(same_owner, before), 1, 0), axis=1).astype(jnp.int32)
    slot_index = owners * capacity + rank
    picker = (
        lax.broadcasted_iota(jnp.int32, (nreq * capacity, pages), 0) == slot_index[None, :]
    ).astype(jnp.bfloat16)
    page_data = jnp.stack([key_hat, values], axis=1).reshape(pages, PAGE * 2 * width_dev)
    outgoing = jnp.dot(picker, page_data, preferred_element_type=jnp.float32).astype(jnp.bfloat16)
    outgoing = outgoing.reshape(nreq * capacity * PAGE, 2, width_dev)
    cache = lax.all_to_all(outgoing, "req", split_axis=0, concat_axis=0, tiled=True)
    query_heads = query_hat.reshape(stream, heads_dev, HEAD)
    key_heads = key_hat.reshape(stream, heads_dev, HEAD)
    value_heads = values.reshape(stream, heads_dev, HEAD)
    self_out = self_attention(query_heads, key_heads, value_heads, segment_ids[0])
    cross_heads = cross_hat.reshape(stream, heads_dev, HEAD)
    prompt_start = prompt_of[0] * TEXT
    gathered = lax.all_gather(text_ready, ("req", "tp"), axis=0, tiled=True)
    prompt_rows = lax.dynamic_slice_in_dim(gathered, prompt_start, TEXT, 0)
    head_start = lax.axis_index("tp") * width_dev
    prompt_rows = lax.dynamic_slice_in_dim(prompt_rows, head_start, width_dev, 2)
    cross_out = cross_attention(cross_heads, prompt_rows)
    return (self_out, cross_out, cache)


def solution(mesh):
    placed = (
        P("req", "tp"),
        P("req", "tp"),
        P("req", "tp"),
        P("req", "tp"),
        P(("req", "tp"), None, None),
        P("req", None),
        P("req"),
        P("req", None),
    )
    return jax.shard_map(
        per_device,
        mesh=mesh,
        in_specs=placed,
        out_specs=(P("req", "tp"), P("req", "tp"), P("req", None, "tp")),
        check_vma=False,
    )
```

profile of v0, /device:TPU:64, one launch (start us, length us, event | category | flops | bytes accessed | tf_op | source)
XLA Modules:
  0.0 517.8 jit_solution(12269761902777181673)
XLA Ops:
  9.5 1.6 copy.74
  12.6 1.6 copy.83
  14.2 2.4 copy.77
  16.9 1.6 fusion.16
  18.8 28.2 %all-reduce = (f32[1024]{0:T(1024)S(1)}, f32[1024]{0:T(1024)S(1)}, f32[1024]{0:T(1024)S(1)}) all-reduce(f32[1024]{0:T(1024)S(1)} %fusion.16, f32[1024]{0:T(1024)S(1)} %fusion.18, f32[1024]{0:T(1024)S(1)} %fusion.20), channel_id=1, replica_groups=mesh['req'=32,'tp'=8] {'tp'}, use_global_device_ids=true, to_apply=%region_1.0 | all-reduce | flops 3072 | bytes 24576 | tf_op jit(solution)/shard_map/psum | solution.py:101
  48.4 1.7 pad_maximum_fusion
  50.1 7.5 %copy.98 = bf16[1024,2,640]{2,1,0:T(2,128)(2,1)} copy(bf16[1024,2,640]{0,2,1:T(8,128)(2,1)} %pad_maximum_fusion) | data formatting | bytes 5242880 | tf_op jit(solution)/shard_map/stack | solution.py:123
  57.6 5.0 reshape.137
  62.8 4.9 convolution_convert_fusion
  67.6 6.8 %reshape.138 = bf16[1536,2,640]{2,1,0:T(2,128)(2,1)} reshape(bf16[96,20480]{1,0:T(8,128)(2,1)} %convolution_convert_fusion) | data formatting | bytes 7864320 | tf_op jit(solution)/shard_map/reshape | solution.py:125
  74.4 7.9 %all-to-all-start = ((bf16[1536,2,640]{2,1,0:T(2,128)(2,1)}), bf16[1536,2,640]{2,1,0:T(2,128)(2,1)}, u32[]{:S(2)}, u32[]{:S(2)}) async-start(bf16[1536,2,640]{2,1,0:T(2,128)(2,1)} %reshape.138), calls=%async_computation | async-start | bytes 7864320 | tf_op jit(solution)/shard_map/all_to_all | solution.py:126
  82.4 2.7 fusion.17
  88.1 2.3 fusion
  90.4 2.3 fusion.1
  92.7 6.9 %fusion.2 = (f32[5,512]{1,0:T(8,128)S(1)}, f32[5,512]{1,0:T(8,128)S(1)}) fusion(f32[5,512,1024]{2,1,0:T(8,128)S(1)} %get-tuple-element.30, f32[5,512]{1,0:T(8,128)S(1)} %broadcast_maximum_fusion.3, pred[512,1024]{1,0:T(8,128)(4,1)S(1)} %get-tuple-element.23, f32[5,512]{1,0:T(8,128)S(1)} %broadcast_maximum_fusion.2, f32[5,512,1024]{2,1,0:T(8,128)S(1)} %get-tuple-element.28, ...), kind=kLoop, calls=%fused_computation.7 | loop fusion | flops 26209280 | bytes 22061056 | tf_op jit(solution)/shard_map/reduce_sum | solution.py:41
  99.7 3.3 divide_convert_fusion.3
  103.0 3.3 divide_convert_fusion.2
  107.8 2.4 copy.99
  110.7 24.5 %all-to-all-done = bf16[1536,2,640]{2,1,0:T(2,128)(2,1)} async-done(((bf16[1536,2,640]{2,1,0:T(2,128)(2,1)}), bf16[1536,2,640]{2,1,0:T(2,128)(2,1)}, u32[]{:S(2)}, u32[]{:S(2)}) %all-to-all-start) | async-done | bytes 3932192 | tf_op jit(solution)/shard_map/all_to_all | solution.py:126
  135.2 344.2 %all-gather.2.cloned.1.call-done = bf16[1024,2,5120]{2,1,0:T(2,128)(2,1)} async-done(((bf16[4,2,5120]{2,1,0:T(2,128)(2,1)}), bf16[1024,2,5120]{2,1,0:T(2,128)(2,1)}) %all-gather.2.cloned.1.call-update) | async-done | bytes 20971536 | tf_op jit(solution)/shard_map/all_gather | solution.py:133
  479.4 7.7 %constant_dynamic-slice_fusion = (bf16[512,1,640]{2,1,0:T(2,128)(2,1)}, bf16[512,1,640]{2,1,0:T(2,128)(2,1)S(1)}) fusion(bf16[1024,2,5120]{2,1,0:T(2,128)(2,1)} %all-gather.2.cloned.1.call-done, s32[]{:T(128)S(6)} %select_n.37, s32[]{:T(128)S(6)} %select_n.39, s32[]{:T(128)S(6)} %add.45), kind=kLoop, calls=%fused_computation.69 | loop fusion | bytes 2621452 | tf_op jit(solution)/shard_map/slice | solution.py:78
  487.1 2.5 copy.118
  489.7 3.2 multiply_reduce_fusion.1
  503.5 7.5 %copy.124 = bf16[1536,2,640]{2,1,0:T(2,128)(2,1)} copy(bf16[1536,2,640]{2,1,0:T(2,128)(2,1)} %all-to-all-done) | data formatting | bytes 7864320
  (51 shorter events, 20.7 us)
Async XLA Ops:
  7.2 3.9 copy-start.3
  7.2 472.2 %all-gather.2.cloned.1.call-start = ((), (), s32[]{:S(2)}) async-start(), calls=%async_computation.1 | async-start | bytes 21053440 | tf_op jit(solution)/shard_map/all_gather | solution.py:133
  47.1 1.3 copy-start.1
  57.6 5.0 copy-start.5
  74.4 60.8 %all-to-all-start = ((bf16[1536,2,640]{2,1,0:T(2,128)(2,1)}), bf16[1536,2,640]{2,1,0:T(2,128)(2,1)}, u32[]{:S(2)}, u32[]{:S(2)}) async-start(bf16[1536,2,640]{2,1,0:T(2,128)(2,1)} %reshape.138), calls=%async_computation | async-start | bytes 7864320 | tf_op jit(solution)/shard_map/all_to_all | solution.py:126
  82.3 3.4 copy-start.4
  92.7 7.0 %copy-start.2 = (bf16[1024,640]{0,1:T(8,128)(2,1)S(1)}, bf16[1024,640]{0,1:T(8,128)(2,1)}, u32[]{:S(2)}) copy-start(bf16[1024,640]{0,1:T(8,128)(2,1)} %copy.77) | copy-start | bytes 3932164
  493.9 2.5 copy-start
Sparse Core Ops, SparseCore 0:
  9.9 469.4 all-gather.1
where the time goes:
time: 519 us; the launch traced here: 518 us
  waiting for transfers between devices  369 us (71%)
  local copies, waits for them, and re-layouts  57 us (11%)
  blocking collectives  28.2 us (5%)
  matrix products  23.3 us (4%)
  other arithmetic  17.7 us (3%)
  between operations  15 us (3%)
  starting transfers between devices  7.92 us (2%)
    all_gather x1, waiting for transfers between devices, per_device(): gathered = lax.all_gather(text_ready, ('req', 'tp'), axis=0, tiled=True)  344 us
    psum x1, blocking collectives, per_device(): lax.psum((square_sums(queries), square_sums(keys), square_sums(cross_quer...  28.2 us
    unnamed x22, local copies, waits for them, and re-layouts  24.6 us
    all_to_all x1, waiting for transfers between devices, per_device(): lax.all_to_all(outgoing, 'req', split_axis=0, concat_axis=0, tiled=True)  24.5 us
  transfers between devices with their start and end apart: 2, of which 2 were waited for; matrix products, arithmetic and copies ran while one was open for 12% of the time, Pallas kernels for 0%

commit v1 on v0

v1 whole, which is shorter than its diff:
```python
import functools
import math

import jax
import jax.numpy as jnp
import numpy as np
from jax import lax
from jax.experimental import pallas as pl
from jax.experimental.layout import Layout, with_layout_constraint
from jax.experimental.pallas import tpu as pltpu
from jax.sharding import PartitionSpec as P

HEADS = 40
HEAD = 128
TEXT = 512
PAGE = 16
CAP = 3
NREQ = 32
NTP = 8
STREAM = 1024
PAGES = STREAM // PAGE
LOCAL = HEADS // NTP
WIDTH = HEADS * HEAD
EPSILON = 1e-06
NEGATIVE = -1e30
MESH = pl.DeviceIdType.MESH
TOK = 4
PART = 48
QBLOCK = 256


def page_order():
    rows = 2 * LOCAL * PAGE
    place = np.zeros((rows, rows), np.float32)
    for token in range(PAGE):
        for head in range(LOCAL):
            for kv in range(2):
                place[(token * LOCAL + head) * 2 + kv, (head * 2 + kv) * PAGE + token] = 1
    return place


def split_order():
    place = np.zeros((NTP * PART, TOK * HEADS * 2), np.float32)
    for part in range(NTP):
        for kv in range(2):
            for head in range(LOCAL):
                for token in range(TOK):
                    row = part * PART + (kv * LOCAL + head) * TOK + token
                    place[row, (token * HEADS + part * LOCAL + head) * 2 + kv] = 1
    return place


def join_order():
    place = np.zeros((2 * LOCAL * NTP * TOK, NTP * PART), np.float32)
    for part in range(NTP):
        for lead in range(2 * LOCAL):
            for token in range(TOK):
                place[lead * NTP * TOK + part * TOK + token, part * PART + lead * TOK + token] = 1
    return place


def kernel(
    source_ref, prompt_ref, q_hbm, k_hbm, v_hbm, c_hbm, text_hbm, seg_ref, page_ref, split_ref, join_ref,
    cache_ref, self_ref, cross_ref,
    q5, k5, v5, c5, text, sums, factor, part_out, part_in, text_k, text_v, outgoing, segcol, bias,
    load_sem, store_sem, sum_send, sum_recv, part_send, part_recv,
    k1_send, k1_recv, v1_send, v1_recv, k2_send, k2_recv, v2_send, v2_recv, page_send, page_recv,
):
    req = lax.axis_index("req")
    tp = lax.axis_index("tp")
    z, x, y = req // 16, (req // 4) % 4, req % 4

    def at(dz, dx, dy):
        return ((z + dz) % 2) * 16 + ((x + dx) % 4) * 4 + (y + dy) % 4

    def remote(src, dst, send, recv, req_to, tp_to):
        return pltpu.make_async_remote_copy(
            src_ref=src, dst_ref=dst, send_sem=send, recv_sem=recv,
            device_id=(req_to, tp_to), device_id_type=MESH,
        )

    def load(index, src, dst):
        copy = pltpu.make_async_copy(src, dst, load_sem.at[index])
        copy.start()
        return copy

    text_load = load(0, text_hbm, text)
    loads = []
    for which, (hbm, buf) in enumerate(((k_hbm, k5), (q_hbm, q5), (c_hbm, c5), (v_hbm, v5))):
        for h in range(LOCAL):
            loads.append(
                load(1 + which * LOCAL + h, hbm.at[:, :, pl.ds(h * HEAD, HEAD)], buf.at[h, pl.ds(0, PAGES)])
            )

    barrier = pltpu.get_barrier_semaphore()

    @pl.loop(1, NREQ)
    def _(d):
        pl.semaphore_signal(barrier, inc=1, device_id=((req + d) % NREQ, tp), device_id_type=MESH)

    @pl.loop(1, NTP)
    def _(d):
        pl.semaphore_signal(barrier, inc=1, device_id=(req, (tp + d) % NTP), device_id_type=MESH)

    for h in range(LOCAL):
        k5[h, PAGES] = jnp.zeros((PAGE, HEAD), jnp.bfloat16)
        v5[h, PAGES] = jnp.zeros((PAGE, HEAD), jnp.bfloat16)

    text_load.wait()
    per = HEADS * 2
    even = lax.broadcasted_iota(jnp.int32, (per, HEAD), 0) % 2 == 0
    normed = []
    for token in range(TOK):
        rows = text[token * per : (token + 1) * per, :].astype(jnp.float32)
        keyed = jnp.where(even, rows, 0.0)
        total = jnp.sum(jnp.sum(keyed * keyed, axis=0, keepdims=True), axis=1, keepdims=True)
        scaled = rows * lax.rsqrt(total / WIDTH + EPSILON)
        normed.append(jnp.where(even, scaled, rows).astype(jnp.bfloat16))
    parts = jnp.dot(split_ref[...], jnp.concatenate(normed, axis=0), preferred_element_type=jnp.float32)
    part_out[...] = parts.astype(jnp.bfloat16).reshape(NTP, PART, HEAD)
    part_in[tp] = part_out[tp]

    pl.semaphore_wait(barrier, NREQ - 1 + NTP - 1)

    def part_copy(d):
        other = (tp + d) % NTP
        return remote(part_out.at[other], part_in.at[tp], part_send.at[d], part_recv.at[d], req, other)

    @pl.loop(1, NTP)
    def _(d):
        part_copy(d).start()

    for which, buf in enumerate((k5, q5, c5)):
        for h in range(LOCAL):
            loads[which * LOCAL + h].wait()

        @pl.loop(0, 8)
        def _(b, which=which, buf=buf):
            acc = jnp.zeros((128, HEAD), jnp.float32)
            for h in range(LOCAL):
                wide = buf[h, pl.ds(b * 8, 8)].reshape(128, HEAD).astype(jnp.float32)
                acc = acc + wide * wide
            sums[tp, which, pl.ds(b, 1), :] = jnp.sum(acc.T, axis=0, keepdims=True)

    def sum_copy(d):
        other = (tp + d) % NTP
        return remote(sums.at[tp], sums.at[tp], sum_send.at[d], sum_recv.at[d], req, other)

    @pl.loop(1, NTP)
    def _(d):
        sum_copy(d).start()

    @pl.loop(1, NTP)
    def _(d):
        part_copy(d).wait()

    block = jnp.dot(join_ref[...], part_in[...].reshape(NTP * PART, HEAD), preferred_element_type=jnp.float32)
    block = block.astype(jnp.bfloat16)
    half = LOCAL * NTP * TOK
    text_k[z, x, y] = block[:half]
    text_v[z, x, y] = block[half:]

    def k1_copy(d):
        own = text_k.at[z, x, y]
        return remote(own, own, k1_send.at[d], k1_recv.at[d], at(d // 4, d % 4, 0), tp)

    def v1_copy(d):
        own = text_v.at[z, x, y]
        return remote(own, own, v1_send.at[d], v1_recv.at[d], at(d // 4, 0, d % 4), tp)

    def k2_copy(d, e):
        held = text_k.at[(z - d // 4 + 2) % 2, (x - d % 4 + 4) % 4, y]
        spot = d * 3 + e - 1
        return remote(held, held, k2_send.at[spot], k2_recv.at[spot], at(0, 0, e), tp)

    def v2_copy(d, e):
        held = text_v.at[(z - d // 4 + 2) % 2, x, (y - d % 4 + 4) % 4]
        spot = d * 3 + e - 1
        return remote(held, held, v2_send.at[spot], v2_recv.at[spot], at(0, e, 0), tp)

    @pl.loop(1, 8)
    def _(d):
        k1_copy(d).start()
        v1_copy(d).start()

    @pl.loop(1, NTP)
    def _(d):
        sum_copy(d).wait()

    total = sums[0]
    for t in range(1, NTP):
        total = total + sums[t]
    factor[...] = lax.rsqrt(total / WIDTH + EPSILON)

    def normalize(which, buf):
        @pl.loop(0, 8)
        def _(b):
            column = jnp.broadcast_to(factor[which, pl.ds(b, 1), :], (128, HEAD)).T
            for h in range(LOCAL):
                wide = buf[h, pl.ds(b * 8, 8)].reshape(128, HEAD).astype(jnp.float32)
                buf[h, pl.ds(b * 8, 8)] = (wide * column).astype(jnp.bfloat16).reshape(8, PAGE, HEAD)

    normalize(0, k5)
    for h in range(LOCAL):
        loads[3 * LOCAL + h].wait()

    @pl.loop(0, 8)
    def _(d):
        @pl.when(d > 0)
        def _():
            k1_copy(d).wait()
            v1_copy(d).wait()

        for e in range(1, 4):
            k2_copy(d, e).start()
            v2_copy(d, e).start()

    def dest(i):
        d = (i * 11) % NREQ
        return at(d // 16, (d // 4) % 4, d % 4), d

    def build(i):
        to, _ = dest(i)
        for j in range(CAP):
            slot = to * CAP + j
            page = source_ref[slot]
            rows = jnp.concatenate([buf[h, page] for h in range(LOCAL) for buf in (k5, v5)], axis=0)
            placed = jnp.dot(page_ref[...], rows, preferred_element_type=jnp.float32)
            outgoing[slot] = placed.astype(jnp.bfloat16)

    def page_copy(i, j):
        to, d = dest(i)
        return remote(
            outgoing.at[to * CAP + j], cache_ref.at[req * CAP + j],
            page_send.at[d * CAP + j], page_recv.at[d * CAP + j], to, tp,
        )

    build(0)
    own = pltpu.make_async_copy(
        outgoing.at[pl.ds(req * CAP, CAP)], cache_ref.at[pl.ds(req * CAP, CAP)], store_sem.at[2 * LOCAL]
    )
    build(1)
    own.start()

    @pl.loop(1, NREQ - 1)
    def _(i):
        build(i + 1)
        for j in range(CAP):
            page_copy(i, j).start()

    normalize(1, q5)
    for j in range(CAP):
        page_copy(NREQ - 1, j).start()
    normalize(2, c5)

    power = HEAD ** (-0.5) * math.log2(math.e)
    qpages = QBLOCK // PAGE

    def soften(scores, values):
        top = jnp.max(scores, axis=1, keepdims=True)
        weights = jnp.exp2(scores - top)
        total = jnp.sum(weights, axis=1, keepdims=True)
        product = jnp.dot(weights.astype(jnp.bfloat16), values, preferred_element_type=jnp.float32)
        return (product / total).astype(jnp.bfloat16)

    for b in range(8):
        lane = seg_ref[:, b * 128 : (b + 1) * 128].astype(jnp.float32)
        segcol[b * 128 : (b + 1) * 128, :] = jnp.broadcast_to(lane, (128, 128)).T

    contract = (((1,), (1,)), ((), ()))

    @pl.loop(0, STREAM // QBLOCK)
    def _(b):
        mine = segcol[pl.ds(b * QBLOCK, QBLOCK), :]
        for j in range(STREAM // 128):
            lane = seg_ref[:, j * 128 : (j + 1) * 128].astype(jnp.float32)
            bias[:, j * 128 : (j + 1) * 128] = jnp.where(mine == lane, 0.0, NEGATIVE)

        @pl.loop(0, LOCAL)
        def _(h):
            rows = q5[h, pl.ds(b * qpages, qpages)].reshape(QBLOCK, HEAD)
            keys = k5[h, pl.ds(0, PAGES)].reshape(STREAM, HEAD)
            scores = lax.dot_general(rows, keys, contract, preferred_element_type=jnp.float32)
            done = soften(scores * power + bias[...], v5[h, pl.ds(0, PAGES)].reshape(STREAM, HEAD))
            q5[h, pl.ds(b * qpages, qpages)] = done.reshape(qpages, PAGE, HEAD)

    stores = []
    for h in range(LOCAL):
        copy = pltpu.make_async_copy(q5.at[h], self_ref.at[:, :, pl.ds(h * HEAD, HEAD)], store_sem.at[h])
        copy.start()
        stores.append(copy)

    @pl.loop(0, 8)
    def _(d):
        for e in range(1, 4):
            k2_copy(d, e).wait()
            v2_copy(d, e).wait()

    prompt = prompt_ref[0]

    @pl.loop(0, STREAM // QBLOCK)
    def _(b):
        @pl.loop(0, LOCAL)
        def _(h):
            tokens = NTP * TOK
            keys = text_k[prompt, :, :, pl.ds(h * tokens, tokens)].reshape(TEXT, HEAD)
            values = text_v[prompt, :, :, pl.ds(h * tokens, tokens)].reshape(TEXT, HEAD)
            rows = c5[h, pl.ds(b * qpages, qpages)].reshape(QBLOCK, HEAD)
            scores = lax.dot_general(rows, keys, contract, preferred_element_type=jnp.float32)
            done = soften(scores * power, values)
            c5[h, pl.ds(b * qpages, qpages)] = done.reshape(qpages, PAGE, HEAD)

    for h in range(LOCAL):
        copy = pltpu.make_async_copy(c5.at[h], cross_ref.at[:, :, pl.ds(h * HEAD, HEAD)], store_sem.at[LOCAL + h])
        copy.start()
        stores.append(copy)

    @pl.loop(1, NREQ)
    def _(i):
        for j in range(CAP):
            page_copy(i, j).wait()

    own.wait()
    for copy in stores:
        copy.wait()


def per_device(queries, keys, values, cross_queries, text_kv, segment_ids, prompt_of, page_owner):
    owners = page_owner[:, 0]
    before = lax.broadcasted_iota(jnp.int32, (PAGES, PAGES), 1) < lax.broadcasted_iota(
        jnp.int32, (PAGES, PAGES), 0
    )
    same = owners[:, None] == owners[None, :]
    rank = jnp.sum(jnp.where(jnp.logical_and(same, before), 1, 0), axis=1).astype(jnp.int32)
    slot = owners * CAP + rank
    hit = lax.broadcasted_iota(jnp.int32, (NREQ * CAP, PAGES), 0) == slot[None, :]
    number = lax.broadcasted_iota(jnp.int32, (NREQ * CAP, PAGES), 1)
    source = PAGES + jnp.sum(jnp.where(hit, number - PAGES, 0), axis=1).astype(jnp.int32)

    paged = lambda a: a.reshape(PAGES, PAGE, LOCAL * HEAD)
    text = text_kv.reshape(TOK, 2, HEADS, HEAD).transpose(0, 2, 1, 3).reshape(TOK * HEADS * 2, HEAD)
    consts = [jnp.asarray(make(), jnp.bfloat16) for make in (page_order, split_order, join_order)]
    rows = PAGE * LOCAL * 2
    out = jax.ShapeDtypeStruct((PAGES, PAGE, LOCAL * HEAD), jnp.bfloat16)
    hbm = pl.BlockSpec(memory_space=pltpu.HBM)
    vmem = pl.BlockSpec(memory_space=pltpu.VMEM)
    smem = pl.BlockSpec(memory_space=pltpu.SMEM)
    dma = lambda count: pltpu.SemaphoreType.DMA((count,))
    heads = lambda pages: pltpu.VMEM((LOCAL, pages, PAGE, HEAD), jnp.bfloat16)
    block = pltpu.VMEM((2, 4, 4, LOCAL * NTP * TOK, HEAD), jnp.bfloat16)
    cache, self_out, cross_out = pl.pallas_call(
        kernel,
        out_shape=(jax.ShapeDtypeStruct((NREQ * CAP, rows, HEAD), jnp.bfloat16), out, out),
        in_specs=[smem, smem, hbm, hbm, hbm, hbm, hbm, vmem, vmem, vmem, vmem],
        out_specs=(hbm, hbm, hbm),
        scratch_shapes=[
            heads(PAGES), heads(PAGES + 1), heads(PAGES + 1), heads(PAGES),
            pltpu.VMEM((TOK * HEADS * 2, HEAD), jnp.bfloat16),
            pltpu.VMEM((NTP, 3, 8, 128), jnp.float32),
            pltpu.VMEM((3, 8, 128), jnp.float32),
            pltpu.VMEM((NTP, PART, HEAD), jnp.bfloat16),
            pltpu.VMEM((NTP, PART, HEAD), jnp.bfloat16),
            block, block,
            pltpu.VMEM((NREQ * CAP, rows, HEAD), jnp.bfloat16),
            pltpu.VMEM((STREAM, 128), jnp.float32),
            pltpu.VMEM((QBLOCK, STREAM), jnp.float32),
            dma(1 + 4 * LOCAL), dma(2 * LOCAL + 1), dma(NTP), dma(NTP), dma(NTP), dma(NTP),
            dma(8), dma(8), dma(8), dma(8), dma(24), dma(24), dma(24), dma(24),
            dma(NREQ * CAP), dma(NREQ * CAP),
        ],
        compiler_params=pltpu.CompilerParams(
            collective_id=0, has_side_effects=True, vmem_limit_bytes=56 * 2**20
        ),
    )(
        source, prompt_of, paged(queries), paged(keys), paged(values), paged(cross_queries), text,
        segment_ids, *consts,
    )
    cache = cache.reshape(NREQ * CAP * PAGE, LOCAL, 2, HEAD).transpose(0, 2, 1, 3)
    cache = with_layout_constraint(cache, Layout(major_to_minor=(0, 2, 1, 3)))
    flat = lambda a: a.reshape(STREAM, LOCAL * HEAD)
    return flat(self_out), flat(cross_out), cache.reshape(NREQ * CAP * PAGE, 2, LOCAL * HEAD)


def solution(mesh):
    placed = (
        P("req", "tp"),
        P("req", "tp"),
        P("req", "tp"),
        P("req", "tp"),
        P(("req", "tp"), None, None),
        P("req", None),
        P("req"),
        P("req", None),
    )
    return jax.shard_map(
        per_device,
        mesh=mesh,
        in_specs=placed,
        out_specs=(P("req", "tp"), P("req", "tp"), P("req", None, "tp")),
        check_vma=False,
    )
```

time: 519 us -> 105 us (0.20)
  waiting for transfers between devices: 369 us -> 0 us
  Pallas kernels: 0 us -> 92.5 us
  local copies, waits for them, and re-layouts: 57 us -> 7.05 us
  blocking collectives: 28.2 us -> 0 us
  matrix products: 23.3 us -> 0 us
  other arithmetic: 17.7 us -> 2.19 us
  between operations: 15 us -> 1.3 us
  starting transfers between devices: 7.92 us -> 0 us
    all_gather x1 -> x0, waiting for transfers between devices: 344 us -> none  [per_device(): gathered = lax.all_gather(text_ready, ('req', 'tp'), axis=0, tiled=True)]
    pallas_call x0 -> x1, Pallas kernels: none -> 92.5 us  [per_device(): pl.pallas_call(kernel, out_shape=(jax.ShapeDtypeStruct((NREQ * CAP, rows,...]
    psum x1 -> x0, blocking collectives: 28.2 us -> none  [per_device(): lax.psum((square_sums(queries), square_sums(keys), square_sums(cross_quer...]
    all_to_all x1 -> x0, waiting for transfers between devices: 24.5 us -> none  [per_device(): lax.all_to_all(outgoing, 'req', split_axis=0, concat_axis=0, tiled=True)]
    dot_general x9 -> x0, matrix products: 23.3 us -> none  [the longest x4 9.79 us: blend(): jnp.einsum('hqk,khe->hqe', weights.astype(jnp.bfloat16), value_part, pref...]
    unnamed x22 -> x5, local copies, waits for them, and re-layouts: 24.6 us -> 7.05 us
    reshape x2 -> x0, local copies, waits for them, and re-layouts: 11.8 us -> none  [the longest x1 6.8 us: per_device(): outgoing = outgoing.reshape(nreq * capacity * PAGE, 2, width_dev)]
    slice x5 -> x0, local copies, waits for them, and re-layouts: 10.4 us -> none  [the longest x1 7.73 us: cross_attention(): key_part = prompt_rows[:, 0, :].reshape(count, heads, depth)]
  transfers between devices with their start and end apart: 2 -> 0, of which waited for: 2 -> 0; matrix products, arithmetic and copies ran while one was open for 12% -> 0% of each run, Pallas kernels for 0% -> 0%
where the time goes in v1:
time: 105 us; the launch traced here: 103 us
  Pallas kernels  92.5 us (88%)
  local copies, waits for them, and re-layouts  7.05 us (7%)
  other arithmetic  2.19 us (2%)
  between operations  1.3 us (1%)
    pallas_call x1, Pallas kernels, per_device(): pl.pallas_call(kernel, out_shape=(jax.ShapeDtypeStruct((NREQ * CAP, rows,...  92.5 us
    unnamed x5, local copies, waits for them, and re-layouts  7.05 us

profile of v1, /device:TPU:64, one launch (start us, length us, event | category | flops | bytes accessed | tf_op | source)
XLA Modules:
  0.0 103.0 jit_solution(14181447455138339429)
XLA Ops:
  1.3 0.9 select_reduce_fusion.1
  2.2 0.7 iota_add_fusion
  2.9 0.1 select_reduce_fusion
  3.0 0.5 broadcast_add_fusion.source_ref
  3.5 92.5 %shard_map.130 = (bf16[96,160,128]{2,1,0:T(8,128)(2,1)}, bf16[64,16,640]{2,1,0:T(8,128)(2,1)}, bf16[64,16,640]{2,1,0:T(8,128)(2,1)}) custom-call(s32[96]{0:T(128)} %broadcast_add_fusion.source_ref, s32[1]{0:T(128)S(6)} %copy.19.prompt_ref, bf16[64,16,640]{2,1,0:T(8,128)(2,1)} %bitcast.21, bf16[64,16,640]{2,1,0:T(8,128)(2,1)} %bitcast.22, ...), custom_call_target="tpu_custom_call" | custom-call | tf_op jit(solution)/shard_map/pallas_call | solution.py:351
  96.0 0.0 copy-start
  96.0 2.6 %copy.20 = bf16[1024,640]{1,0:T(8,128)(2,1)} copy(bf16[1024,640]{1,0:T(8,128)(2,1)} %bitcast.20) | data formatting | bytes 2621440
  98.6 2.5 %copy.21 = bf16[1024,640]{1,0:T(8,128)(2,1)} copy(bf16[1024,640]{1,0:T(8,128)(2,1)} %bitcast.19) | data formatting | bytes 2621440
  101.1 0.0 copy-done
  101.1 1.9 %copy.22 = bf16[1536,2,640]{2,1,0:T(2,128)(2,1)} copy(bf16[1536,2,640]{2,1,0:T(2,128)(2,1)S(1)} %bitcast.18) | data formatting | bytes 7864320
Async XLA Ops:
  96.0 5.1 %copy-start = (bf16[96,160,128]{2,1,0:T(8,128)(2,1)S(1)}, bf16[96,160,128]{2,1,0:T(8,128)(2,1)}, u32[]{:S(2)}) copy-start(bf16[96,160,128]{2,1,0:T(8,128)(2,1)} %get-tuple-element.8) | copy-start | bytes 11796484
